TPU v7x, 32 devices: a whole 2x2x4 slice. The times are simulated.
32 devices in a mesh: aux: 4 (over x, core), orb: 8 (over z, y).
Axes of the slice: x: 2, y: 2, z: 4, core: 2. Of those that a mesh axis runs over, the one named last changes fastest.
Arguments:
- three_center: bfloat16 [640, 8, 3, 4096], P(('aux', 'orb')), may hold values from -1.5 to 1.5
- atom_size: int32 [8], replicated, may hold values from 32 to 64
- tensor_pattern: int32 [40, 8, 3], P('aux', 'orb'), may hold values 0 or 1
- green_occ: bfloat16 [8, 3, 4096], P('orb'), may hold values from -0.5 to 0.5
- green_virt: bfloat16 [8, 3, 4096], P('orb'), may hold values from -0.5 to 0.5
- green_pattern: int32 [8, 3], P('orb'), may hold values 0 or 1
Outputs:
- chi: float32 [640, 640], P(('aux', 'orb'))
Inputs may be any that keep to these rules, and one draw needn't show every extreme that they name: `atom_size`: functions in use per block.
All inputs are finite; a program needn't handle non-finite values. No bound on the sum of `tensor_pattern` or of `green_pattern` on one device may be relied on, other than what follows from the above.
Results may differ from a plain program's by a relative error of at most 0.0041.
Values may be sent and summed in bfloat16 or wider, within the bound.
A program may use at most 128 MiB of HBM per device.

v0:
```python
import functools

import jax
import jax.numpy as jnp
from jax import lax
from jax.experimental import pallas as pl
from jax.experimental.pallas import tpu as pltpu
from jax.sharding import PartitionSpec as P

BS = 64
R = 1
W = 3
ABS = 16
LANES = 128


def block_masks(atom_size, first_block, local_blocks):
    total_blocks = atom_size.shape[0]
    owned = first_block + jnp.arange(local_blocks, dtype=jnp.int32)
    offsets = jnp.arange(W, dtype=jnp.int32)
    partner = owned[:, None] + offsets[None, :] - R
    inside = (partner >= 0) & (partner < total_blocks)
    catalog = jnp.arange(total_blocks, dtype=jnp.int32)
    size_partner = jnp.sum(jnp.where(partner[:, :, None] == catalog, atom_size, 0), axis=2)
    size_owned = jnp.sum(jnp.where(owned[:, None] == catalog, atom_size, 0), axis=1)
    funcs = jnp.arange(BS, dtype=jnp.int32)
    rows_ok = (funcs[None, None, :] < size_partner[:, :, None]) & inside[:, :, None]
    cols_ok = funcs[None, :] < size_owned[:, None]
    pair_ok = rows_ok[:, :, :, None] & cols_ok[:, None, None, :]
    return (inside, pair_ok.reshape(local_blocks, W, BS * BS))


def gather(x, axis):
    count = lax.axis_size(axis)
    return lax.all_to_all(
        jnp.broadcast_to(x[None], (count,) + x.shape), axis, split_axis=0, concat_axis=0, tiled=True
    )


def x_kernel(t_ref, v_ref, o_ref, x_ref, second_ref):
    n = pl.program_id(0)
    blocks = t_ref.shape[0]
    width = t_ref.shape[3]
    tiles = width // LANES
    for e in range(W):
        total = None
        for d in range(W):
            if abs(e - d) <= R:
                m = jnp.clip(n + d - R, 0, blocks - 1)
                block = t_ref[m, e - d + R]
                rows = jnp.concatenate(
                    [block[:, j * LANES : (j + 1) * LANES] for j in range(tiles)], axis=0
                )
                part = jnp.dot(rows, v_ref[0, d], preferred_element_type=jnp.float32)
                total = part if total is None else total + part
        total = total.astype(second_ref.dtype)
        for j in range(tiles):
            second_ref[e * BS : (e + 1) * BS, j * LANES : (j + 1) * LANES] = total[
                j * BS : (j + 1) * BS
            ]
    x_ref[0] = jnp.dot(o_ref[0], second_ref[...], preferred_element_type=jnp.float32).astype(
        x_ref.dtype
    )


def x_products(tensor, virt2, occ_t):
    blocks, _, _, width = tensor.shape
    depth = W * BS
    return pl.pallas_call(
        x_kernel,
        grid=(blocks,),
        in_specs=[
            pl.BlockSpec(tensor.shape, lambda n: (0, 0, 0, 0)),
            pl.BlockSpec((1, W, LANES, LANES), lambda n: (n, 0, 0, 0)),
            pl.BlockSpec((1, depth, depth), lambda n: (n, 0, 0)),
        ],
        out_specs=pl.BlockSpec((1, depth, width), lambda n: (n, 0, 0)),
        out_shape=jax.ShapeDtypeStruct((blocks, depth, width), jnp.bfloat16),
        scratch_shapes=[pltpu.VMEM((depth, width), jnp.bfloat16)],
        cost_estimate=pl.CostEstimate(
            flops=blocks * width * (7 * BS * LANES * 2 + depth * depth * 2),
            bytes_accessed=tensor.size * 4,
            transcendentals=0,
        ),
    )(tensor, virt2, occ_t)


def send_kernel(share, first, t_ref, pair_ref, row_ref, out_ref):
    blocks = t_ref.shape[1]
    size = t_ref.shape[3]
    targets = out_ref.shape[0]
    for n in range(blocks):
        for d in range(W):
            b = n * W + d
            begin, end = max(b * size, first), min((b + 1) * size, first + targets * share)
            if begin >= end:
                continue
            kept = row_ref[:, b : b + 1] * pair_ref[b : b + 1, :]
            block = t_ref[:, n, d, :] * kept
            while begin < end:
                target = (begin - first) // share
                stop = min(end, first + (target + 1) * share)
                at = begin - first - target * share
                out_ref[target, :, at : at + stop - begin] = block[
                    :, begin - b * size : stop - b * size
                ]
                begin = stop


def send_layout(three_center, pair, row, targets, share, first):
    rows = three_center.shape[0]
    return pl.pallas_call(
        functools.partial(send_kernel, share, first),
        in_specs=[pl.BlockSpec(memory_space=pltpu.VMEM)] * 3,
        out_specs=pl.BlockSpec(memory_space=pltpu.VMEM),
        out_shape=jax.ShapeDtypeStruct((targets, rows, share), jnp.bfloat16),
        compiler_params=pltpu.CompilerParams(vmem_limit_bytes=48 << 20),
    )(three_center, pair, row)


def chi_kernel(left_ref, right_ref, out_ref, l_ref, r_ref):
    sources, rows, _ = right_ref.shape
    for s in range(sources):
        l_ref[s * rows : (s + 1) * rows, :] = left_ref[s]
        r_ref[s * rows : (s + 1) * rows, :] = right_ref[s]
    out_ref[...] = lax.dot_general(
        l_ref[...], r_ref[...], (((1,), (1,)), ((), ())), preferred_element_type=jnp.float32
    ).astype(out_ref.dtype)


def chi_part(left, right):
    sources, rows, share = right.shape
    functions = sources * rows
    return pl.pallas_call(
        chi_kernel,
        in_specs=[pl.BlockSpec(memory_space=pltpu.VMEM)] * 2,
        out_specs=pl.BlockSpec(memory_space=pltpu.VMEM),
        out_shape=jax.ShapeDtypeStruct((functions, functions), jnp.bfloat16),
        scratch_shapes=[pltpu.VMEM((functions, share), jnp.bfloat16)] * 2,
        compiler_params=pltpu.CompilerParams(vmem_limit_bytes=56 << 20),
    )(left, right)


def body(three_center, atom_size, tensor_pattern, green_occ, green_virt, green_pattern):
    both = ("aux", "orb")
    n_aux, n_orb = lax.axis_size("aux"), lax.axis_size("orb")
    orb = lax.axis_index("orb")
    rows, blocks = three_center.shape[0], three_center.shape[1]
    local_blocks = green_occ.shape[0]
    area = BS * BS
    targets = n_aux * n_orb
    width = rows * BS
    total = blocks * W * area
    trim = area if (total - 2 * area) % (targets * LANES) == 0 else 0
    share = (total - 2 * trim) // targets

    inside, pair_ok = block_masks(atom_size, orb * local_blocks, local_blocks)
    diagonal = jnp.arange(W, dtype=jnp.int32) == R
    green_keep = ((green_pattern > 0) | diagonal[None, :]) & inside
    green_mask = green_keep[..., None] & pair_ok
    occ = jnp.where(green_mask, green_occ, jnp.zeros((), green_occ.dtype))
    virt = jnp.where(green_mask, green_virt, jnp.zeros((), green_virt.dtype))
    pattern = (tensor_pattern > 0).astype(jnp.bfloat16)
    groups = pattern.shape[0]
    pattern_orb = gather(pattern, "orb").transpose(1, 0, 2, 3).reshape(groups, blocks * W)
    greens = jnp.concatenate([occ, virt], axis=1)

    _, pair_all = block_masks(atom_size, jnp.int32(0), blocks)
    pair_all = pair_all.reshape(blocks * W, area).astype(jnp.bfloat16)
    rows_here = jnp.repeat(pattern_orb, ABS, axis=0)
    rows_here = lax.dynamic_slice_in_dim(rows_here, orb * rows, rows, axis=0)
    outgoing = send_layout(three_center, pair_all, rows_here, targets, share, trim)
    left = lax.all_to_all(outgoing, both, split_axis=0, concat_axis=0, tiled=True)

    gathered = gather(greens, "orb").reshape(blocks, 2 * W, BS, BS)
    occ_all, virt_all = gathered[:, :W], gathered[:, W:]

    turned = outgoing.reshape(targets, rows, share // BS, BS).transpose(0, 2, 1, 3)
    tensor = turned.reshape(targets * share // BS, width)
    tensor = jnp.pad(tensor, ((trim // BS, trim // BS), (0, 0))).reshape(blocks, W, BS, width)
    zero = jnp.zeros_like(virt_all)
    virt2 = jnp.concatenate(
        [jnp.concatenate([virt_all, zero], axis=3), jnp.concatenate([zero, virt_all], axis=3)],
        axis=2,
    )
    occ_pad = jnp.pad(occ_all, ((R, R), (0, 0), (0, 0), (0, 0)))
    none = jnp.zeros((blocks, BS, BS), occ_all.dtype)
    occ_t = jnp.concatenate(
        [
            jnp.concatenate(
                [
                    occ_pad[d : d + blocks, e - d + R].transpose(0, 2, 1)
                    if abs(e - d) <= R
                    else none
                    for e in range(W)
                ],
                axis=2,
            )
            for d in range(W)
        ],
        axis=1,
    )
    x = x_products(tensor, virt2, occ_t).reshape(total // BS, width)
    x = x[trim // BS : (total - trim) // BS]
    x = x.reshape(targets, share // BS, rows, BS).transpose(0, 2, 1, 3).reshape(targets, rows, share)
    right = lax.all_to_all(x, both, split_axis=0, concat_axis=0, tiled=True)

    part = chi_part(left, right)
    functions = part.shape[0]
    part = part.reshape(n_aux, functions // n_aux, functions)
    part = lax.all_to_all(part, "aux", split_axis=0, concat_axis=0, tiled=True)
    part = jnp.sum(part.astype(jnp.float32), axis=0).astype(jnp.bfloat16)
    part = part.reshape(n_orb, rows, functions)
    part = lax.all_to_all(part, "orb", split_axis=0, concat_axis=0, tiled=True)
    return jnp.sum(part.astype(jnp.float32), axis=0)


def solution(mesh):
    return jax.shard_map(
        body,
        mesh=mesh,
        in_specs=(
            P(("aux", "orb"), None, None, None),
            P(),
            P("aux", "orb", None),
            P("orb", None, None),
            P("orb", None, None),
            P("orb", None),
        ),
        out_specs=P(("aux", "orb"), None),
        check_vma=False,
    )
```

profile of v0, /device:TPU:0, one launch (start us, length us, event | category | flops | bytes accessed | tf_op | source)
XLA Modules:
  0.0 285.5 jit_solution(3773173451904322098)
XLA Ops:
  0.0 0.7 compare_convert_fusion
  0.7 0.6 broadcast_in_dim.92
  1.3 7.3 %all-to-all-start = ((bf16[8,10,1,3]{1,3,2,0:T(4,128)(2,1)}), bf16[8,10,1,3]{1,3,2,0:T(4,128)(2,1)S(1)}, u32[]{:S(2)}, u32[]{:S(2)}) async-start(bf16[8,10,1,3]{1,3,2,0:T(4,128)(2,1)} %broadcast_in_dim.92), calls=%async_computation | async-start | bytes 16384 | tf_op jit(solution)/shard_map/all_to_all | solution.py:35
  8.6 0.8 select_reduce_fusion.1
  9.4 1.4 fusion.10
  10.8 0.9 select_reduce_fusion
  11.7 0.9 fusion.9
  12.5 0.1 fusion.8
  12.6 0.1 and.129
  12.7 0.1 and.130
  12.8 0.7 iota_compare_fusion.7
  13.6 0.1 and.132
  13.6 0.7 and_bitcast_fusion
  14.3 0.9 broadcast_select_fusion.1
  15.2 7.9 %copy.37.t_ref = bf16[20,8,3,4096]{3,2,1,0:T(4,128)(2,1)} copy(bf16[20,8,3,4096]{3,1,2,0:T(8,128)(2,1)} %param.6) | data formatting | bytes 7864320 | tf_op args[0]
  23.2 0.1 copy.34
  23.3 0.1 copy.35
  23.4 0.0 all-to-all-done
  23.4 0.8 broadcast_in_dim.99
  24.2 6.0 %all-to-all-start.2 = ((bf16[8,1,6,4096]{3,2,1,0:T(8,128)(2,1)}), bf16[8,1,6,4096]{3,2,1,0:T(8,128)(2,1)S(1)}, u32[]{:S(2)}, u32[]{:S(2)}) async-start(bf16[8,1,6,4096]{3,2,1,0:T(8,128)(2,1)} %broadcast_in_dim.99), calls=%async_computation.2 | async-start | bytes 1048576 | tf_op jit(solution)/shard_map/all_to_all | solution.py:35
  30.2 0.1 iota_compare_fusion.5
  30.3 0.1 fusion.7
  30.4 0.3 and_convert_fusion
  30.6 0.4 reshape.333.pair_ref
  31.0 0.1 copy.36
  31.2 10.9 %shard_map.64 = bf16[32,20,2816]{2,1,0:T(8,128)(2,1)S(1)} custom-call(bf16[20,8,3,4096]{3,2,1,0:T(4,128)(2,1)} %copy.37.t_ref, bf16[24,4096]{1,0:T(8,128)(2,1)S(1)} %reshape.333.pair_ref, bf16[20,24]{1,0:T(8,128)(2,1)S(1)} %constant_dynamic-slice_fusion.row_ref), custom_call_target="tpu_custom_call" | custom-call | tf_op jit(solution)/shard_map/pallas_call | solution.py:112
  42.0 0.0 copy-start
  42.0 2.0 copy-done
  44.0 0.1 all-to-all-done.2
  44.2 6.2 %all-to-all-start.1 = ((bf16[32,20,2816]{2,1,0:T(8,128)(2,1)}), bf16[32,20,2816]{2,1,0:T(8,128)(2,1)}, u32[]{:S(2)}, u32[]{:S(2)}) async-start(bf16[32,20,2816]{2,1,0:T(8,128)(2,1)} %copy-done), calls=%async_computation.1 | async-start | bytes 8650752 | tf_op jit(solution)/shard_map/all_to_all | solution.py:173
  50.4 4.7 %copy.38 = bf16[32,20,2816]{2,0,1:T(8,128)(2,1)} copy(bf16[32,20,2816]{2,1,0:T(8,128)(2,1)} %copy-done) | data formatting | bytes 7208960 | tf_op jit(solution)/shard_map/pallas_call | solution.py:112
  55.1 10.6 %reshape.324 = bf16[32,20,44,64]{3,2,0,1:T(8,128)(2,1)} reshape(bf16[32,20,2816]{2,0,1:T(8,128)(2,1)} %copy.38) | data formatting | bytes 7208960 | tf_op jit(solution)/shard_map/reshape | solution.py:178
  65.7 14.3 %copy.39 = bf16[32,44,20,64]{3,2,1,0:T(8,128)(2,1)} copy(bf16[32,44,20,64]{3,1,0,2:T(8,128)(2,1)} %bitcast.50) | data formatting | bytes 7208960 | tf_op jit(solution)/shard_map/transpose | solution.py:178
  80.0 11.0 %reshape.325 = bf16[1408,1280]{1,0:T(8,128)(2,1)} reshape(bf16[32,44,20,64]{3,2,1,0:T(8,128)(2,1)} %copy.39) | data formatting | bytes 7208960 | tf_op jit(solution)/shard_map/reshape | solution.py:179
  91.0 4.2 %pad.10 = bf16[1536,1280]{1,0:T(8,128)(2,1)} pad(bf16[1408,1280]{1,0:T(8,128)(2,1)} %reshape.325, bf16[]{:T(256)} %constant.15.clone.1), padding=64_64x0_0 | pad | bytes 7536642 | tf_op jit(solution)/shard_map/jit(_pad)/pad | solution.py:180
  95.2 0.2 copy.40
  95.4 0.8 reshape.327
  96.3 0.1 fusion.12
  96.3 0.2 copy.52
  96.6 0.1 copy.55
  96.7 0.1 copy.54
  96.9 0.1 copy.53
  97.0 0.1 fusion.3
  97.1 1.3 maximum_maximum_fusion.o_ref
  98.5 1.2 fusion.2.v_ref
  99.7 10.2 %shard_map.65 = bf16[8,192,1280]{2,1,0:T(8,128)(2,1)} custom-call(bf16[8,3,64,1280]{3,2,1,0:T(8,128)(2,1)} %bitcast.51, bf16[8,3,128,128]{3,2,1,0:T(8,128)(2,1)} %fusion.2.v_ref, bf16[8,192,192]{2,1,0:T(8,128)(2,1)} %maximum_maximum_fusion.o_ref), custom_call_target="tpu_custom_call" | custom-call | flops 1929379840 | bytes 7864320 | tf_op jit(solution)/shard_map/pallas_call | solution.py:69
  109.8 4.0 %slice.51 = bf16[1408,1280]{1,0:T(8,128)(2,1)} slice(bf16[1536,1280]{1,0:T(8,128)(2,1)} %bitcast.52), slice={[64:1472], [0:1280]} | slice | bytes 7208960 | tf_op jit(solution)/shard_map/slice | solution.py:204
  113.9 11.3 %reshape.329 = bf16[32,44,20,64]{3,2,1,0:T(8,128)(2,1)} reshape(bf16[1408,1280]{1,0:T(8,128)(2,1)} %slice.51) | data formatting | bytes 7208960 | tf_op jit(solution)/shard_map/reshape | solution.py:205
  125.2 8.2 %copy.48 = bf16[32,20,44,64]{3,2,1,0:T(8,128)(2,1)} copy(bf16[32,20,44,64]{3,1,2,0:T(8,128)(2,1)} %bitcast.49) | data formatting | bytes 7208960 | tf_op jit(solution)/shard_map/reshape | solution.py:205
  133.4 11.4 %reshape.335 = bf16[32,20,2816]{2,1,0:T(8,128)(2,1)} reshape(bf16[32,20,44,64]{3,2,1,0:T(8,128)(2,1)} %copy.48) | data formatting | bytes 7208960 | tf_op jit(solution)/shard_map/reshape | solution.py:205
  144.8 4.0 %all-to-all-done.1.left_ref = bf16[32,20,2816]{2,1,0:T(8,128)(2,1)} async-done(((bf16[32,20,2816]{2,1,0:T(8,128)(2,1)}), bf16[32,20,2816]{2,1,0:T(8,128)(2,1)}, u32[]{:S(2)}, u32[]{:S(2)}) %all-to-all-start.1) | async-done | bytes 3604512 | tf_op jit(solution)/shard_map/all_to_all | solution.py:173
  148.8 101.2 %all_to_all.30.right_ref = bf16[32,20,2816]{2,1,0:T(8,128)(2,1)} all-to-all(bf16[32,20,2816]{2,1,0:T(8,128)(2,1)} %reshape.335), channel_id=1, replica_groups=mesh['aux'=4,'orb'=8] {'aux','orb'}, dimensions={0} | all-to-all | bytes 7208960 | tf_op jit(solution)/shard_map/all_to_all | solution.py:206
  250.0 7.5 %shard_map.66 = bf16[640,640]{1,0:T(8,128)(2,1)} custom-call(bf16[32,20,2816]{2,1,0:T(8,128)(2,1)} %all-to-all-done.1.left_ref, bf16[32,20,2816]{2,1,0:T(8,128)(2,1)} %all_to_all.30.right_ref), custom_call_target="tpu_custom_call" | custom-call | tf_op jit(solution)/shard_map/pallas_call | solution.py:134
  257.6 15.4 %all_to_all.31 = bf16[4,160,640]{2,1,0:T(8,128)(2,1)S(1)} all-to-all(bf16[4,160,640]{2,1,0:T(8,128)(2,1)} %bitcast.53), channel_id=1, replica_groups=mesh['aux'=4,'orb'=8] {'aux'}, dimensions={0} | all-to-all | bytes 1638400 | tf_op jit(solution)/shard_map/all_to_all | solution.py:211
  273.0 0.1 reduce_sum.61
  273.2 11.7 %all_to_all.32 = bf16[8,20,640]{2,1,0:T(8,128)(2,1)S(1)} all-to-all(bf16[8,20,640]{2,1,0:T(8,128)(2,1)S(1)} %reshape.332), channel_id=1, replica_groups=mesh['aux'=4,'orb'=8] {'orb'}, dimensions={0} | all-to-all | bytes 409600 | tf_op jit(solution)/shard_map/all_to_all | solution.py:214
  284.9 0.7 convert_reduce_fusion
  (13 shorter events, 0.2 us)
Async XLA Ops:
  1.3 22.1 %all-to-all-start = ((bf16[8,10,1,3]{1,3,2,0:T(4,128)(2,1)}), bf16[8,10,1,3]{1,3,2,0:T(4,128)(2,1)S(1)}, u32[]{:S(2)}, u32[]{:S(2)}) async-start(bf16[8,10,1,3]{1,3,2,0:T(4,128)(2,1)} %broadcast_in_dim.92), calls=%async_computation | async-start | bytes 16384 | tf_op jit(solution)/shard_map/all_to_all | solution.py:35
  24.2 19.9 %all-to-all-start.2 = ((bf16[8,1,6,4096]{3,2,1,0:T(8,128)(2,1)}), bf16[8,1,6,4096]{3,2,1,0:T(8,128)(2,1)S(1)}, u32[]{:S(2)}, u32[]{:S(2)}) async-start(bf16[8,1,6,4096]{3,2,1,0:T(8,128)(2,1)} %broadcast_in_dim.99), calls=%async_computation.2 | async-start | bytes 1048576 | tf_op jit(solution)/shard_map/all_to_all | solution.py:35
  42.0 2.0 copy-start
  44.2 104.6 %all-to-all-start.1 = ((bf16[32,20,2816]{2,1,0:T(8,128)(2,1)}), bf16[32,20,2816]{2,1,0:T(8,128)(2,1)}, u32[]{:S(2)}, u32[]{:S(2)}) async-start(bf16[32,20,2816]{2,1,0:T(8,128)(2,1)} %copy-done), calls=%async_computation.1 | async-start | bytes 8650752 | tf_op jit(solution)/shard_map/all_to_all | solution.py:173
where the time goes:
time: 288 us; the launch traced here: 286 us
  blocking collectives  128 us (44%)
  local copies, waits for them, and re-layouts  94.1 us (33%)
  Pallas kernels  28.6 us (10%)
  starting transfers between devices  19.5 us (7%)
  other arithmetic  10.7 us (4%)
  waiting for transfers between devices  4.13 us (1%)
    all_to_all x1, blocking collectives, body(): right = lax.all_to_all(x, both, split_axis=0, concat_axis=0, tiled=True)  101 us
    reshape x3, local copies, waits for them, and re-layouts, body(): x.reshape(targets, share // BS, rows, BS).transpose(0, 2, 1, 3)  30.9 us
    all_to_all x1, blocking collectives, body(): part = lax.all_to_all(part, 'aux', split_axis=0, concat_axis=0, tiled=True)  15.4 us
    transpose x1, local copies, waits for them, and re-layouts, body(): outgoing.reshape(targets, rows, share // BS, BS).transpose(0, 2, 1, 3)  14.3 us
    all_to_all x2, starting transfers between devices, gather(): lax.all_to_all(jnp.broadcast_to(x[None], (count,) + x.shape), axis, split...  13.3 us
    all_to_all x1, blocking collectives, body(): part = lax.all_to_all(part, 'orb', split_axis=0, concat_axis=0, tiled=True)  11.7 us
    reshape x1, local copies, waits for them, and re-layouts, body(): tensor = turned.reshape(targets * share // BS, width)  11 us
    pallas_call x1, Pallas kernels, send_layout(): pl.pallas_call(functools.partial(send_kernel, share, first), in_specs=[pl...  10.9 us
  transfers between devices with their start and end apart: 3, of which 2 were waited for; matrix products, arithmetic and copies ran while one was open for 35% of the time, Pallas kernels for 7%

commit v1 on v0

--- a/solution.py
+++ b/solution.py
@@ -86,7 +86,7 @@
 
 
 def send_kernel(share, first, t_ref, pair_ref, row_ref, out_ref):
-    blocks = t_ref.shape[1]
+    blocks = t_ref.shape[2]
     size = t_ref.shape[3]
     targets = out_ref.shape[0]
     for n in range(blocks):
@@ -96,7 +96,7 @@
             if begin >= end:
                 continue
             kept = row_ref[:, b : b + 1] * pair_ref[b : b + 1, :]
-            block = t_ref[:, n, d, :] * kept
+            block = t_ref[:, d, n, :] * kept
             while begin < end:
                 target = (begin - first) // share
                 stop = min(end, first + (target + 1) * share)
@@ -115,7 +115,7 @@
         out_specs=pl.BlockSpec(memory_space=pltpu.VMEM),
         out_shape=jax.ShapeDtypeStruct((targets, rows, share), jnp.bfloat16),
         compiler_params=pltpu.CompilerParams(vmem_limit_bytes=48 << 20),
-    )(three_center, pair, row)
+    )(three_center.transpose(0, 2, 1, 3), pair, row)
 
 
 def chi_kernel(left_ref, right_ref, out_ref, l_ref, r_ref):
@@ -154,26 +154,36 @@
     trim = area if (total - 2 * area) % (targets * LANES) == 0 else 0
     share = (total - 2 * trim) // targets
 
-    inside, pair_ok = block_masks(atom_size, orb * local_blocks, local_blocks)
-    diagonal = jnp.arange(W, dtype=jnp.int32) == R
-    green_keep = ((green_pattern > 0) | diagonal[None, :]) & inside
-    green_mask = green_keep[..., None] & pair_ok
-    occ = jnp.where(green_mask, green_occ, jnp.zeros((), green_occ.dtype))
-    virt = jnp.where(green_mask, green_virt, jnp.zeros((), green_virt.dtype))
-    pattern = (tensor_pattern > 0).astype(jnp.bfloat16)
-    groups = pattern.shape[0]
-    pattern_orb = gather(pattern, "orb").transpose(1, 0, 2, 3).reshape(groups, blocks * W)
-    greens = jnp.concatenate([occ, virt], axis=1)
-
-    _, pair_all = block_masks(atom_size, jnp.int32(0), blocks)
-    pair_all = pair_all.reshape(blocks * W, area).astype(jnp.bfloat16)
+    groups = tensor_pattern.shape[0]
+    flags = jnp.concatenate([tensor_pattern.reshape(-1), green_pattern.reshape(-1)])
+    flags = (flags > 0).astype(jnp.bfloat16)
+    counts = (groups * local_blocks * W, local_blocks * W)
+    lines = -(-flags.shape[0] // area)
+    flags = jnp.pad(flags, (0, lines * area - flags.shape[0])).reshape(lines, area)
+    packed = jnp.concatenate(
+        [green_occ.reshape(-1, area), green_virt.reshape(-1, area), flags], axis=0
+    )
+    packed = gather(packed, "orb")
+    flags = packed[:, 2 * local_blocks * W :].reshape(n_orb, lines * area)
+    pattern_orb = flags[:, : counts[0]].reshape(n_orb, groups, local_blocks, W)
+    pattern_orb = pattern_orb.transpose(1, 0, 2, 3).reshape(groups, blocks * W)
+    green_all = flags[:, counts[0] : counts[0] + counts[1]].reshape(blocks, W)
+
+    inside, pair_ok = block_masks(atom_size, jnp.int32(0), blocks)
+    pair_all = pair_ok.reshape(blocks * W, area).astype(jnp.bfloat16)
     rows_here = jnp.repeat(pattern_orb, ABS, axis=0)
     rows_here = lax.dynamic_slice_in_dim(rows_here, orb * rows, rows, axis=0)
     outgoing = send_layout(three_center, pair_all, rows_here, targets, share, trim)
     left = lax.all_to_all(outgoing, both, split_axis=0, concat_axis=0, tiled=True)
 
-    gathered = gather(greens, "orb").reshape(blocks, 2 * W, BS, BS)
-    occ_all, virt_all = gathered[:, :W], gathered[:, W:]
+    diagonal = jnp.arange(W, dtype=jnp.int32) == R
+    green_keep = ((green_all > 0) | diagonal[None, :]) & inside
+    green_mask = (green_keep[..., None] & pair_ok).reshape(blocks, W, BS, BS)
+    half = local_blocks * W
+    occ_all = packed[:, :half].reshape(blocks, W, BS, BS)
+    virt_all = packed[:, half : 2 * half].reshape(blocks, W, BS, BS)
+    occ_all = jnp.where(green_mask, occ_all, jnp.zeros((), occ_all.dtype))
+    virt_all = jnp.where(green_mask, virt_all, jnp.zeros((), virt_all.dtype))
 
     turned = outgoing.reshape(targets, rows, share // BS, BS).transpose(0, 2, 1, 3)
     tensor = turned.reshape(targets * share // BS, width)

time: 288 us -> 279 us (0.969)
  waiting for transfers between devices: 4.13 us -> 16.4 us
  starting transfers between devices: 19.5 us -> 11.3 us
  local copies, waits for them, and re-layouts: 94.1 us -> 87.9 us
  other arithmetic: 10.7 us -> 5.17 us
    all_to_all x2 -> x1, waiting for transfers between devices: 0.12 us -> 13 us  [gather(): lax.all_to_all(jnp.broadcast_to(x[None], (count,) + x.shape), axis, split...]
    unnamed x8 -> x6, local copies, waits for them, and re-layouts: 10.6 us -> 2.97 us
    all_to_all x2 -> x1, starting transfers between devices: 13.3 us -> 7.31 us  [gather(): lax.all_to_all(jnp.broadcast_to(x[None], (count,) + x.shape), axis, split...]
  transfers between devices with their start and end apart: 3 -> 2, of which waited for: 2 -> 2; matrix products, arithmetic and copies ran while one was open for 35% -> 31% of each run, Pallas kernels for 7% -> 4%
where the time goes in v1:
time: 279 us; the launch traced here: 277 us
  blocking collectives  128 us (46%)
  local copies, waits for them, and re-layouts  87.9 us (32%)
  Pallas kernels  27.4 us (10%)
  waiting for transfers between devices  16.4 us (6%)
  starting transfers between devices  11.3 us (4%)
  other arithmetic  5.17 us (2%)
    all_to_all x1, blocking collectives, body(): right = lax.all_to_all(x, both, split_axis=0, concat_axis=0, tiled=True)  101 us
    reshape x3, local copies, waits for them, and re-layouts, body(): x.reshape(targets, share // BS, rows, BS).transpose(0, 2, 1, 3)  30.9 us
    all_to_all x1, blocking collectives, body(): part = lax.all_to_all(part, 'aux', split_axis=0, concat_axis=0, tiled=True)  15.4 us
    transpose x1, local copies, waits for them, and re-layouts, body(): outgoing.reshape(targets, rows, share // BS, BS).transpose(0, 2, 1, 3)  14.3 us
    all_to_all x1, waiting for transfers between devices, gather(): lax.all_to_all(jnp.broadcast_to(x[None], (count,) + x.shape), axis, split...  13 us
    all_to_all x1, blocking collectives, body(): part = lax.all_to_all(part, 'orb', split_axis=0, concat_axis=0, tiled=True)  11.7 us
    reshape x1, local copies, waits for them, and re-layouts, body(): tensor = turned.reshape(targets * share // BS, width)  11 us
    reshape x1, local copies, waits for them, and re-layouts, body(): outgoing.reshape(targets, rows, share // BS, BS).transpose(0, 2, 1, 3)  10.6 us
  transfers between devices with their start and end apart: 2, of which 2 were waited for; matrix products, arithmetic and copies ran while one was open for 31% of the time, Pallas kernels for 4%

profile of v1, /device:TPU:0, one launch (start us, length us, event | category | flops | bytes accessed | tf_op | source)
XLA Modules:
  0.0 276.6 jit_solution(13263967751031592584)
XLA Ops:
  0.0 0.0 copy-start.1
  0.0 0.8 copy.61
  0.8 0.1 reshape.126
  0.9 0.7 add_compare_fusion
  1.6 0.8 pad_maximum_fusion
  2.5 0.8 broadcast_in_dim.30
  3.3 7.3 %all-to-all-start = ((bf16[8,7,4096]{2,1,0:T(8,128)(2,1)}), bf16[8,7,4096]{2,1,0:T(8,128)(2,1)S(1)}, u32[]{:S(2)}, u32[]{:S(2)}) async-start(bf16[8,7,4096]{2,1,0:T(8,128)(2,1)} %broadcast_in_dim.30), calls=%async_computation | async-start | bytes 1048576 | tf_op jit(solution)/shard_map/all_to_all | solution.py:35
  10.6 0.0 copy-done.1
  10.6 0.1 select_reduce_fusion.1
  10.7 0.1 copy.58
  10.8 0.1 copy.59
  10.9 0.2 select_reduce_fusion
  11.1 0.1 iota_compare_fusion.5
  11.2 0.1 fusion.9
  11.3 0.2 and_convert_fusion
  11.5 0.2 copy.60
  11.7 0.4 reshape.144.pair_ref
  12.1 13.0 %all-to-all-done = bf16[8,7,4096]{2,1,0:T(8,128)(2,1)S(1)} async-done(((bf16[8,7,4096]{2,1,0:T(8,128)(2,1)}), bf16[8,7,4096]{2,1,0:T(8,128)(2,1)S(1)}, u32[]{:S(2)}, u32[]{:S(2)}) %all-to-all-start) | async-done | bytes 458784 | tf_op jit(solution)/shard_map/all_to_all | solution.py:35
  25.1 0.1 slice.55
  25.2 0.1 copy.84
  25.3 0.1 copy.63
  25.4 0.1 copy.64
  25.6 0.1 copy.65
  25.7 0.0 copy-start
  25.7 2.1 copy-done
  27.8 9.7 %shard_map.64 = bf16[32,20,2816]{2,1,0:T(8,128)(2,1)} custom-call(bf16[20,3,8,4096]{3,2,1,0:T(8,128)(2,1)S(1)} %bitcast.52, bf16[24,4096]{1,0:T(8,128)(2,1)S(1)} %reshape.144.pair_ref, bf16[20,24]{1,0:T(8,128)(2,1)S(1)} %constant_dynamic-slice_fusion.row_ref), custom_call_target="tpu_custom_call" | custom-call | tf_op jit(solution)/shard_map/pallas_call | solution.py:112
  37.5 3.9 %all-to-all-start.1 = ((bf16[32,20,2816]{2,1,0:T(8,128)(2,1)}), bf16[32,20,2816]{2,1,0:T(8,128)(2,1)}, u32[]{:S(2)}, u32[]{:S(2)}) async-start(bf16[32,20,2816]{2,1,0:T(8,128)(2,1)} %shard_map.64), calls=%async_computation.1 | async-start | bytes 8650752 | tf_op jit(solution)/shard_map/all_to_all | solution.py:177
  41.5 4.7 %copy.66 = bf16[32,20,2816]{2,0,1:T(8,128)(2,1)} copy(bf16[32,20,2816]{2,1,0:T(8,128)(2,1)} %shard_map.64) | data formatting | bytes 7208960 | tf_op jit(solution)/shard_map/pallas_call | solution.py:112
  46.2 10.6 %reshape.134 = bf16[32,20,44,64]{3,2,0,1:T(8,128)(2,1)} reshape(bf16[32,20,2816]{2,0,1:T(8,128)(2,1)} %copy.66) | data formatting | bytes 7208960 | tf_op jit(solution)/shard_map/reshape | solution.py:188
  56.8 14.3 %copy.67 = bf16[32,44,20,64]{3,2,1,0:T(8,128)(2,1)} copy(bf16[32,44,20,64]{3,1,0,2:T(8,128)(2,1)} %bitcast.54) | data formatting | bytes 7208960 | tf_op jit(solution)/shard_map/transpose | solution.py:188
  71.1 11.0 %reshape.135 = bf16[1408,1280]{1,0:T(8,128)(2,1)} reshape(bf16[32,44,20,64]{3,2,1,0:T(8,128)(2,1)} %copy.67) | data formatting | bytes 7208960 | tf_op jit(solution)/shard_map/reshape | solution.py:189
  82.1 0.2 fusion.10
  82.4 0.4 reshape.148
  82.8 0.2 copy.72
  83.0 0.1 or_and_fusion
  83.1 0.1 copy.68
  83.2 0.4 reshape.147
  83.5 0.2 copy.70
  83.8 0.4 fusion.2
  84.2 0.3 fusion.4
  84.5 1.2 copy.73.v_ref
  85.7 4.2 %pad.16 = bf16[1536,1280]{1,0:T(8,128)(2,1)} pad(bf16[1408,1280]{1,0:T(8,128)(2,1)} %reshape.135, bf16[]{:T(256)} %constant.7.clone.1), padding=64_64x0_0 | pad | bytes 7536642 | tf_op jit(solution)/shard_map/jit(_pad)/pad | solution.py:190
  89.9 0.2 fusion.5
  90.0 1.4 maximum_maximum_fusion.o_ref
  91.4 10.2 %shard_map.65 = bf16[8,192,1280]{2,1,0:T(8,128)(2,1)} custom-call(bf16[8,3,64,1280]{3,2,1,0:T(8,128)(2,1)} %bitcast.55, bf16[8,3,128,128]{3,2,1,0:T(8,128)(2,1)} %copy.73.v_ref, bf16[8,192,192]{2,1,0:T(8,128)(2,1)} %maximum_maximum_fusion.o_ref), custom_call_target="tpu_custom_call" | custom-call | flops 1929379840 | bytes 7864320 | tf_op jit(solution)/shard_map/pallas_call | solution.py:69
  101.6 4.0 %slice.63 = bf16[1408,1280]{1,0:T(8,128)(2,1)} slice(bf16[1536,1280]{1,0:T(8,128)(2,1)} %bitcast.56), slice={[64:1472], [0:1280]} | slice | bytes 7208960 | tf_op jit(solution)/shard_map/slice | solution.py:214
  105.6 11.3 %reshape.140 = bf16[32,44,20,64]{3,2,1,0:T(8,128)(2,1)} reshape(bf16[1408,1280]{1,0:T(8,128)(2,1)} %slice.63) | data formatting | bytes 7208960 | tf_op jit(solution)/shard_map/reshape | solution.py:215
  116.9 8.2 %copy.80 = bf16[32,20,44,64]{3,2,1,0:T(8,128)(2,1)} copy(bf16[32,20,44,64]{3,1,2,0:T(8,128)(2,1)} %bitcast.53) | data formatting | bytes 7208960 | tf_op jit(solution)/shard_map/reshape | solution.py:215
  125.2 11.4 %reshape.149 = bf16[32,20,2816]{2,1,0:T(8,128)(2,1)} reshape(bf16[32,20,44,64]{3,2,1,0:T(8,128)(2,1)} %copy.80) | data formatting | bytes 7208960 | tf_op jit(solution)/shard_map/reshape | solution.py:215
  136.5 3.4 %all-to-all-done.1.left_ref = bf16[32,20,2816]{2,1,0:T(8,128)(2,1)} async-done(((bf16[32,20,2816]{2,1,0:T(8,128)(2,1)}), bf16[32,20,2816]{2,1,0:T(8,128)(2,1)}, u32[]{:S(2)}, u32[]{:S(2)}) %all-to-all-start.1) | async-done | bytes 3604512 | tf_op jit(solution)/shard_map/all_to_all | solution.py:177
  139.9 101.2 %all_to_all.25.right_ref = bf16[32,20,2816]{2,1,0:T(8,128)(2,1)} all-to-all(bf16[32,20,2816]{2,1,0:T(8,128)(2,1)} %reshape.149), channel_id=1, replica_groups=mesh['aux'=4,'orb'=8] {'aux','orb'}, dimensions={0} | all-to-all | bytes 7208960 | tf_op jit(solution)/shard_map/all_to_all | solution.py:216
  241.2 7.5 %shard_map.66 = bf16[640,640]{1,0:T(8,128)(2,1)} custom-call(bf16[32,20,2816]{2,1,0:T(8,128)(2,1)} %all-to-all-done.1.left_ref, bf16[32,20,2816]{2,1,0:T(8,128)(2,1)} %all_to_all.25.right_ref), custom_call_target="tpu_custom_call" | custom-call | tf_op jit(solution)/shard_map/pallas_call | solution.py:134
  248.7 15.4 %all_to_all.26 = bf16[4,160,640]{2,1,0:T(8,128)(2,1)S(1)} all-to-all(bf16[4,160,640]{2,1,0:T(8,128)(2,1)} %bitcast.57), channel_id=1, replica_groups=mesh['aux'=4,'orb'=8] {'aux'}, dimensions={0} | all-to-all | bytes 1638400 | tf_op jit(solution)/shard_map/all_to_all | solution.py:221
  264.1 0.1 reduce_sum.41
  264.3 11.7 %all_to_all.27 = bf16[8,20,640]{2,1,0:T(8,128)(2,1)S(1)} all-to-all(bf16[8,20,640]{2,1,0:T(8,128)(2,1)S(1)} %reshape.143), channel_id=1, replica_groups=mesh['aux'=4,'orb'=8] {'orb'}, dimensions={0} | all-to-all | bytes 409600 | tf_op jit(solution)/shard_map/all_to_all | solution.py:224
  276.0 0.7 convert_reduce_fusion
  (12 shorter events, 0.2 us)
Async XLA Ops:
  0.0 10.6 %copy-start.1 = (s32[8]{0:T(128)S(1)}, s32[8]{0:T(128)}, u32[]{:S(2)}) copy-start(s32[8]{0:T(128)} %param.7) | copy-start | bytes 100
  3.3 21.8 %all-to-all-start = ((bf16[8,7,4096]{2,1,0:T(8,128)(2,1)}), bf16[8,7,4096]{2,1,0:T(8,128)(2,1)S(1)}, u32[]{:S(2)}, u32[]{:S(2)}) async-start(bf16[8,7,4096]{2,1,0:T(8,128)(2,1)} %broadcast_in_dim.30), calls=%async_computation | async-start | bytes 1048576 | tf_op jit(solution)/shard_map/all_to_all | solution.py:35
  25.7 2.1 copy-start
  37.5 102.4 %all-to-all-start.1 = ((bf16[32,20,2816]{2,1,0:T(8,128)(2,1)}), bf16[32,20,2816]{2,1,0:T(8,128)(2,1)}, u32[]{:S(2)}, u32[]{:S(2)}) async-start(bf16[32,20,2816]{2,1,0:T(8,128)(2,1)} %shard_map.64), calls=%async_computation.1 | async-start | bytes 8650752 | tf_op jit(solution)/shard_map/all_to_all | solution.py:177
